TPU v7x, 128 devices: a whole 4x4x4 slice. The times are simulated.
128 devices in a mesh: tok: 16 (over z, x_hi, core), req: 8 (over x_lo, y).
Axes of the slice: x: 4 (x_hi: 2, x_lo: 2; x = x_hi * 2 + x_lo), y: 4, z: 4, core: 2. Of those that a mesh axis runs over, the one named last changes fastest.
Arguments:
- query_rows: bfloat16 [8, 4096, 7168], P('req', 'tok'), may hold values from -16 to 16
- key_rows: bfloat16 [8, 4096, 7168], P('req', 'tok'), may hold values from -16 to 16
- value_rows: bfloat16 [8, 4096, 7168], P('req', 'tok'), may hold values from -6 to 6
- lengths: int32 [8, 6], P('req'), may hold values from 1 to 2048, 4096 in all within a row
- cache_blocks: bfloat16 [8, 128, 2, 32, 3584], P('req', 'tok'), may hold values from -6 to 6
- destinations: int32 [8, 128, 1], P('req', 'tok'), may hold values from 0 to 7; in each aligned block of 8 rows (0 to 7, 8 to 15, ..., all dimensions but the last counted through in order) at most 2 rows name the same one
Outputs:
- attended: bfloat16 [8, 4096, 7168], P('req', 'tok')
- moved_cache: bfloat16 [8, 8, 2, 2, 16, 32, 3584], P('req', None, None, None, None, 'tok')
Inputs may be any that keep to these rules, and one draw needn't show every extreme that they name: The 6 lengths of each span sum to 4096, and the longest of every span is exactly 2048. `destinations`: of the 8 rows of one device (aligned blocks of 8 rows), at most 2 name the same group, and in every draw some device names one group exactly 2 times.
All inputs are finite; a program needn't handle non-finite values.
Results may differ from a plain program's by a relative error of at most 0.0037.
Values may be sent and summed in bfloat16 or wider, within the bound.
A program may use at most 192 MiB of HBM per device.

v0:
```python
import jax
import jax.numpy as jnp
from jax import lax
from jax.sharding import PartitionSpec as P

HD = 224
CAP = 2


def segment_ids(lengths_row, span_length):
    ends = jnp.cumsum(lengths_row)
    positions = jnp.arange(span_length, dtype=jnp.int32)
    return jnp.sum((positions[:, None] >= ends[None, :]).astype(jnp.int32), axis=1)


def attend_item(query_all, key_all, value_all, segments):
    length = query_all.shape[0]
    heads_here = query_all.shape[1] // HD
    positions = jnp.arange(length, dtype=jnp.int32)
    block_rows = min(512, length)
    results = []
    for block_start in range(0, length, block_rows):
        block_end = block_start + block_rows
        visible = (segments[block_start:block_end, None] == segments[None, :block_end]) & (
            positions[block_start:block_end, None] >= positions[None, :block_end]
        )
        head_results = []
        for head in range(heads_here):
            low = head * HD
            high = low + HD
            query_block = query_all[block_start:block_end, low:high]
            key_block = key_all[:block_end, low:high]
            value_block = value_all[:block_end, low:high]
            scores = lax.dot_general(
                query_block, key_block, (((1,), (1,)), ((), ())), preferred_element_type=jnp.float32
            ) * HD ** (-0.5)
            scores = jnp.where(visible, scores, -1e30)
            row_max = jnp.max(scores, axis=1, keepdims=True)
            weights = jnp.where(visible, jnp.exp(scores - row_max), 0.0)
            row_total = jnp.sum(weights, axis=1, keepdims=True)
            summed = jnp.dot(
                weights.astype(jnp.bfloat16), value_block, preferred_element_type=jnp.float32
            )
            head_results.append((summed / row_total).astype(jnp.bfloat16))
        results.append(jnp.concatenate(head_results, axis=1))
    return jnp.concatenate(results, axis=0)


def attend_heads(parts, segments):
    query_part, key_part, value_part = parts
    length = query_part.shape[0]
    item_count = query_part.shape[2]
    outputs = [attend_item(query_part[:, 0, 0], key_part[:, 0, 0], value_part[:, 0, 0], segments)]
    return jnp.stack(outputs, axis=1).reshape(length, 1, item_count, query_part.shape[3])


def regroup_attend(query_rows, key_rows, value_rows, segments):
    tok_count = lax.axis_size("tok")
    token_rows = query_rows.shape[1]
    feature_width = query_rows.shape[2]
    group_width = feature_width // tok_count

    def by_group(rows_in):
        return rows_in[0].reshape(token_rows, tok_count, 1, group_width)

    mixed = attend_heads(
        (
            lax.all_to_all(by_group(query_rows), "tok", split_axis=1, concat_axis=0, tiled=True),
            lax.all_to_all(by_group(key_rows), "tok", split_axis=1, concat_axis=0, tiled=True),
            lax.all_to_all(by_group(value_rows), "tok", split_axis=1, concat_axis=0, tiled=True),
        ),
        segments=segments,
    )
    returned = lax.all_to_all(mixed, "tok", split_axis=0, concat_axis=1, tiled=True)
    return returned.reshape(1, token_rows, feature_width)


def relocate(cache_blocks, destinations):
    groups = lax.axis_size("req")
    tok_count = lax.axis_size("tok")
    targets = destinations[0, :, 0]
    block_count = targets.shape[0]
    positions = jnp.arange(block_count, dtype=jnp.int32)
    earlier = (targets[:, None] == targets[None, :]) & (positions[None, :] < positions[:, None])
    slot_rank = jnp.sum(earlier.astype(jnp.int32), axis=1)
    group_ids = jnp.arange(groups, dtype=jnp.int32)
    slot_ids = jnp.arange(CAP, dtype=jnp.int32)
    placing = (
        (targets[:, None, None] == group_ids[None, :, None])
        & (slot_rank[:, None, None] == slot_ids[None, None, :])
    ).astype(cache_blocks.dtype)
    local_blocks = cache_blocks[0]
    heads_all = local_blocks.shape[2]
    local_blocks = local_blocks.reshape(
        block_count, 2, tok_count, heads_all // tok_count, local_blocks.shape[3]
    )
    outgoing = jnp.einsum(
        "bdc,bjthy->dcjthy", placing, local_blocks, preferred_element_type=jnp.float32
    ).astype(jnp.bfloat16)
    arrived = lax.all_to_all(
        lax.all_to_all(outgoing, "tok", split_axis=3, concat_axis=3, tiled=True),
        "req",
        split_axis=0,
        concat_axis=0,
        tiled=True,
    )
    return arrived[None]


def on_device(query_rows, key_rows, value_rows, lengths, cache_blocks, destinations):
    span_length = query_rows.shape[1] * lax.axis_size("tok")
    segments = segment_ids(lengths[0], span_length)
    attended = regroup_attend(query_rows, key_rows, value_rows, segments)
    moved_cache = relocate(cache_blocks, destinations)
    return (attended, moved_cache)


def solution(mesh):
    return jax.shard_map(
        on_device,
        mesh=mesh,
        in_specs=(
            P("req", "tok", None),
            P("req", "tok", None),
            P("req", "tok", None),
            P("req", None),
            P("req", "tok", None, None, None),
            P("req", "tok", None),
        ),
        out_specs=(P("req", "tok", None), P("req", None, None, None, None, "tok", None)),
        check_vma=False,
    )
```

profile of v0, /device:TPU:1, one launch (start us, length us, event | category | flops | bytes accessed | tf_op | source)
XLA Modules:
  0.0 419.9 jit_solution(5922651007471697967)
XLA Ops:
  0.6 5.9 %copy.54 = bf16[1,256,7168]{1,2,0:T(8,128)(2,1)} copy(bf16[1,256,7168]{2,1,0:T(8,128)(2,1)} %param.7) | data formatting | bytes 7340032 | tf_op args[1]
  6.5 9.3 %all-to-all-start.1 = ((bf16[256,16,1,448]{0,3,2,1:T(8,128)(2,1)}), bf16[256,16,1,448]{0,3,2,1:T(8,128)(2,1)}, u32[]{:S(2)}, u32[]{:S(2)}) async-start(bf16[256,16,1,448]{0,3,2,1:T(8,128)(2,1)} %bitcast.60), calls=%async_computation.1 | async-start | bytes 7340032 | tf_op jit(solution)/shard_map/all_to_all | solution.py:69
  15.8 5.9 %copy.51 = bf16[1,256,7168]{1,2,0:T(8,128)(2,1)} copy(bf16[1,256,7168]{2,1,0:T(8,128)(2,1)} %param.6) | data formatting | bytes 7340032 | tf_op args[0]
  21.7 39.6 %all-to-all-done.1 = bf16[256,16,1,448]{0,3,2,1:T(8,128)(2,1)} async-done(((bf16[256,16,1,448]{0,3,2,1:T(8,128)(2,1)}), bf16[256,16,1,448]{0,3,2,1:T(8,128)(2,1)}, u32[]{:S(2)}, u32[]{:S(2)}) %all-to-all-start.1) | async-done | bytes 3670048 | tf_op jit(solution)/shard_map/all_to_all | solution.py:69
  61.3 5.2 %all-to-all-start = ((bf16[256,16,1,448]{0,3,2,1:T(8,128)(2,1)}), bf16[256,16,1,448]{0,3,2,1:T(8,128)(2,1)}, u32[]{:S(2)}, u32[]{:S(2)}) async-start(bf16[256,16,1,448]{0,3,2,1:T(8,128)(2,1)} %bitcast.59), calls=%async_computation | async-start | bytes 7340032 | tf_op jit(solution)/shard_map/all_to_all | solution.py:68
  66.5 5.9 %copy.57 = bf16[1,256,7168]{1,2,0:T(8,128)(2,1)} copy(bf16[1,256,7168]{2,1,0:T(8,128)(2,1)} %param.8) | data formatting | bytes 7340032 | tf_op args[2]
  72.4 5.9 %copy.69 = bf16[1,8,2,32,3584]{4,1,3,2,0:T(8,128)(2,1)} copy(bf16[1,8,2,32,3584]{4,3,2,1,0:T(8,128)(2,1)} %param.10) | data formatting | bytes 7340032 | tf_op jit(solution)/shard_map/reshape;squeeze | solution.py:94
  78.8 7.1 %convolution_convert_fusion = bf16[8,2,2,16,2,3584]{5,0,4,3,2,1:T(8,128)(2,1)} fusion(bf16[8,2,16,2,3584,1]{4,0,3,2,1,5:T(8,128)(2,1)} %bitcast.62, pred[8,2]{0,1:T(4,128)(4,1)S(1)} %iota_compare_fusion.4, pred[8,8]{0,1:T(8,128)(4,1)S(1)} %iota_compare_fusion.3), kind=kOutput, calls=%fused_computation.6 | convolution fusion | flops 62390400 | bytes 11010128 | tf_op jit(solution)/shard_map/bdc,bjthy->dcjthy/dot_general | solution.py:97
  86.0 26.1 %all-to-all-done = bf16[256,16,1,448]{0,3,2,1:T(8,128)(2,1)} async-done(((bf16[256,16,1,448]{0,3,2,1:T(8,128)(2,1)}), bf16[256,16,1,448]{0,3,2,1:T(8,128)(2,1)}, u32[]{:S(2)}, u32[]{:S(2)}) %all-to-all-start) | async-done | bytes 3670048 | tf_op jit(solution)/shard_map/all_to_all | solution.py:68
  112.0 5.8 %all-to-all-start.2 = ((bf16[256,16,1,448]{0,3,2,1:T(8,128)(2,1)}), bf16[256,16,1,448]{0,3,2,1:T(8,128)(2,1)}, u32[]{:S(2)}, u32[]{:S(2)}) async-start(bf16[256,16,1,448]{0,3,2,1:T(8,128)(2,1)} %bitcast.58), calls=%async_computation.2 | async-start | bytes 7340032 | tf_op jit(solution)/shard_map/all_to_all | solution.py:70
  118.0 6.7 %copy.64 = bf16[8,2,2,16,2,3584]{5,0,4,2,1,3:T(8,128)(2,1)} copy(bf16[8,2,2,16,2,3584]{5,0,4,3,2,1:T(8,128)(2,1)} %convolution_convert_fusion) | data formatting | bytes 14680064 | tf_op jit(solution)/shard_map/convert_element_type | solution.py:99
  124.7 2.5 copy.73
  127.2 3.8 copy.72
  134.1 2.6 fusion.303
  137.9 3.5 fusion.305
  141.4 3.4 fusion.306
  144.8 4.5 %fusion.307 = (f32[512]{0:T(512)S(1)}, f32[512,3584]{1,0:T(8,128)}) fusion(bf16[4096,448]{0,1:T(8,128)(2,1)S(1)} %bitcast.78, bf16[4096,448]{0,1:T(8,128)(2,1)S(1)} %bitcast.94, s32[3584]{0:T(1024)S(1)} %iota_add_fusion, s32[512]{0:T(512)S(1)} %iota_add_fusion.7, s32[3584]{0:T(1024)S(1)} %bitcast.120, s32[512]{0:T(512)S(1)} %get-tuple-element.29), kind=kOutput, calls=%fused_computation.282 | convolution fusion | flops 833093120 | bytes 9213952 | tf_op jit(solution)/shard_map/dot_general | solution.py:34
  149.3 4.5 %fusion.308 = (f32[512]{0:T(512)S(1)}, f32[512,3584]{1,0:T(8,128)}) fusion(bf16[4096,448]{0,1:T(8,128)(2,1)S(1)} %bitcast.79, bf16[4096,448]{0,1:T(8,128)(2,1)S(1)} %bitcast.95, s32[3584]{0:T(1024)S(1)} %iota_add_fusion, s32[512]{0:T(512)S(1)} %iota_add_fusion.7, s32[3584]{0:T(1024)S(1)} %bitcast.121, s32[512]{0:T(512)S(1)} %get-tuple-element.29), kind=kOutput, calls=%fused_computation.283 | convolution fusion | flops 833093120 | bytes 9213952 | tf_op jit(solution)/shard_map/dot_general | solution.py:34
  153.8 9.5 %all-to-all-done.2 = bf16[256,16,1,448]{0,3,2,1:T(8,128)(2,1)} async-done(((bf16[256,16,1,448]{0,3,2,1:T(8,128)(2,1)}), bf16[256,16,1,448]{0,3,2,1:T(8,128)(2,1)}, u32[]{:S(2)}, u32[]{:S(2)}) %all-to-all-start.2) | async-done | bytes 3670048 | tf_op jit(solution)/shard_map/all_to_all | solution.py:70
  163.3 5.6 %all-to-all-start.4 = ((bf16[8,2,2,16,2,3584]{5,0,4,2,1,3:T(8,128)(2,1)}), bf16[8,2,2,16,2,3584]{5,0,4,2,1,3:T(8,128)(2,1)}, u32[]{:S(2)}, u32[]{:S(2)}) async-start(bf16[8,2,2,16,2,3584]{5,0,4,2,1,3:T(8,128)(2,1)} %copy.64), calls=%async_computation.4 | async-start | bytes 14680064 | tf_op jit(solution)/shard_map/all_to_all | solution.py:101
  169.0 2.7 copy.71
  181.1 2.2 fusion.53
  187.0 2.4 fusion.49
  195.4 3.6 fusion.27
  204.3 3.4 fusion.31
  207.7 2.3 fusion.33
  212.2 2.2 fusion.116
  218.3 4.5 %fusion.5 = (f32[512]{0:T(512)S(1)}, f32[512]{0:T(512)S(1)}) fusion(f32[512,3584]{1,0:T(8,128)S(1)} %bitcast.65, f32[512]{0:T(512)S(1)} %get-tuple-element.59, s32[3584]{0:T(1024)S(1)} %iota_add_fusion, s32[512]{0:T(512)S(1)} %iota_add_fusion.7, s32[3584]{0:T(1024)S(1)} %bitcast.122, s32[512]{0:T(512)S(1)} %get-tuple-element.29, ...), kind=kLoop, calls=%fused_computation.26 | loop fusion | flops 16514048 | bytes 14721024 | tf_op jit(solution)/shard_map/reduce_sum | solution.py:40
  225.8 2.2 fusion.136
  228.8 2.8 fusion.1
  231.6 4.6 %fusion.9 = (f32[512]{0:T(512)S(1)}, f32[512]{0:T(512)S(1)}, f32[512,4096]{1,0:T(8,128)S(1)}) fusion(f32[512,4096]{1,0:T(8,128)S(1)} %get-tuple-element.62, f32[512]{0:T(512)S(1)} %get-tuple-element.61, s32[512]{0:T(512)S(1)} %iota_add_fusion.6, s32[4096]{0:T(1024)S(1)} %convert_reduce_fusion, s32[512]{0:T(512)S(1)} %get-tuple-element.28, ...), kind=kOutput, calls=%fused_computation.30 | convolution fusion | flops 962591744 | bytes 18868224 | tf_op jit(solution)/shard_map/dot_general | solution.py:34
  236.2 3.4 fusion.11
  239.7 3.0 fusion.166
  242.7 3.0 fusion.156
  246.9 6.2 %reduce = bf16[4096,448]{0,1:T(8,128)(2,1)} reduce(bf16[4096,1,1,448]{0,3,2,1:T(8,128)(2,1)} %bitcast.14, bf16[]{:T(256)} %broadcast.221), dimensions={1,2}, to_apply=%copy.60.reduce_sub_computation | reduce | bytes 7340034 | tf_op jit(solution)/shard_map/reshape;stack | solution.py:54
  253.1 6.3 %copy.77 = bf16[4096,448]{1,0:T(8,128)(2,1)} copy(bf16[4096,448]{0,1:T(8,128)(2,1)} %reduce) | data formatting | bytes 7340032
  259.4 12.3 %reshape.155 = bf16[16,2,57344]{2,1,0:T(2,128)(2,1)} reshape(bf16[4096,448]{1,0:T(8,128)(2,1)} %copy.77) | data formatting | bytes 7340032
  271.8 7.3 %all-to-all-start.3 = ((bf16[16,2,57344]{2,1,0:T(2,128)(2,1)}), bf16[16,2,57344]{2,1,0:T(2,128)(2,1)}, u32[]{:S(2)}, u32[]{:S(2)}) async-start(bf16[16,2,57344]{2,1,0:T(2,128)(2,1)} %reshape.155), calls=%async_computation.3 | async-start | bytes 7340032 | tf_op jit(solution)/shard_map/all_to_all | solution.py:74
  279.0 11.8 %copy.65 = bf16[8,2,2,16,2,3584]{5,4,3,2,1,0:T(2,128)(2,1)} copy(bf16[8,2,2,16,2,3584]{5,0,4,2,1,3:T(8,128)(2,1)} %all-to-all-done.4) | data formatting | bytes 14680064 | tf_op jit(solution)/shard_map/all_to_all | solution.py:101
  290.9 33.7 %all-to-all-done.3 = bf16[16,2,57344]{2,1,0:T(2,128)(2,1)} async-done(((bf16[16,2,57344]{2,1,0:T(2,128)(2,1)}), bf16[16,2,57344]{2,1,0:T(2,128)(2,1)}, u32[]{:S(2)}, u32[]{:S(2)}) %all-to-all-start.3) | async-done | bytes 3670048 | tf_op jit(solution)/shard_map/all_to_all | solution.py:74
  324.5 5.2 %all-to-all-start.5 = ((bf16[8,2,2,16,2,3584]{5,4,3,2,1,0:T(2,128)(2,1)}), bf16[8,2,2,16,2,3584]{5,4,3,2,1,0:T(2,128)(2,1)}, u32[]{:S(2)}, u32[]{:S(2)}) async-start(bf16[8,2,2,16,2,3584]{5,4,3,2,1,0:T(2,128)(2,1)} %copy.65), calls=%async_computation.5 | async-start | bytes 14680064 | tf_op jit(solution)/shard_map/all_to_all | solution.py:100
  329.7 13.2 %reshape.156 = bf16[4096,1,1,448]{3,2,1,0:T(2,128)(2,1)} reshape(bf16[16,2,57344]{2,1,0:T(2,128)(2,1)} %all-to-all-done.3) | data formatting | bytes 7340032
  342.9 6.6 %copy.70 = bf16[4096,1,1,448]{3,0,1,2:T(8,128)(2,1)} copy(bf16[4096,1,1,448]{3,2,1,0:T(2,128)(2,1)} %reshape.156) | data formatting | bytes 7340032
  349.5 7.7 %copy.68 = bf16[16,256,1,1,448]{1,0,4,3,2:T(8,128)(2,1)} copy(bf16[16,256,1,1,448]{4,1,0,3,2:T(8,128)(2,1)} %bitcast.57) | data formatting | bytes 7340032 | tf_op jit(solution)/shard_map/all_to_all | solution.py:74
  357.2 5.1 %copy.62 = bf16[256,16,1,1,448]{0,4,1,3,2:T(8,128)(2,1)} copy(bf16[256,16,1,1,448]{0,1,4,3,2:T(8,128)(2,1)} %bitcast.63) | data formatting | bytes 7340032 | tf_op jit(solution)/shard_map/all_to_all | solution.py:74
  362.3 5.9 %copy.66 = bf16[1,256,7168]{2,1,0:T(8,128)(2,1)} copy(bf16[1,256,7168]{1,2,0:T(8,128)(2,1)} %bitcast.61) | data formatting | bytes 7340032
  368.2 43.8 %all-to-all-done.5 = bf16[8,2,2,16,2,3584]{5,4,3,2,1,0:T(2,128)(2,1)} async-done(((bf16[8,2,2,16,2,3584]{5,4,3,2,1,0:T(2,128)(2,1)}), bf16[8,2,2,16,2,3584]{5,4,3,2,1,0:T(2,128)(2,1)}, u32[]{:S(2)}, u32[]{:S(2)}) %all-to-all-start.5) | async-done | bytes 7340064 | tf_op jit(solution)/shard_map/all_to_all | solution.py:100
  412.1 7.6 %copy.86 = bf16[1,8,2,2,16,2,3584]{6,5,4,3,2,1,0:T(2,128)(2,1)} copy(bf16[1,8,2,2,16,2,3584]{6,5,4,3,2,1,0:T(2,128)(2,1)} %bitcast.22) | data formatting | bytes 14680064
  (95 shorter events, 40.0 us)
Async XLA Ops:
  6.5 54.8 %all-to-all-start.1 = ((bf16[256,16,1,448]{0,3,2,1:T(8,128)(2,1)}), bf16[256,16,1,448]{0,3,2,1:T(8,128)(2,1)}, u32[]{:S(2)}, u32[]{:S(2)}) async-start(bf16[256,16,1,448]{0,3,2,1:T(8,128)(2,1)} %bitcast.60), calls=%async_computation.1 | async-start | bytes 7340032 | tf_op jit(solution)/shard_map/all_to_all | solution.py:69
  61.3 50.7 %all-to-all-start = ((bf16[256,16,1,448]{0,3,2,1:T(8,128)(2,1)}), bf16[256,16,1,448]{0,3,2,1:T(8,128)(2,1)}, u32[]{:S(2)}, u32[]{:S(2)}) async-start(bf16[256,16,1,448]{0,3,2,1:T(8,128)(2,1)} %bitcast.59), calls=%async_computation | async-start | bytes 7340032 | tf_op jit(solution)/shard_map/all_to_all | solution.py:68
  72.4 5.9 %copy-start.7 = (s32[1,6]{1,0:T(1,128)S(1)}, s32[1,6]{1,0:T(1,128)}, u32[]{:S(2)}) copy-start(s32[1,6]{1,0:T(1,128)} %param.9) | copy-start | bytes 76
  72.4 6.2 %copy-start.8 = (s32[1,8,1]{1,2,0:T(1,128)S(1)}, s32[1,8,1]{1,2,0:T(1,128)}, u32[]{:S(2)}) copy-start(s32[1,8,1]{1,2,0:T(1,128)} %param.11) | copy-start | bytes 100
  112.0 51.3 %all-to-all-start.2 = ((bf16[256,16,1,448]{0,3,2,1:T(8,128)(2,1)}), bf16[256,16,1,448]{0,3,2,1:T(8,128)(2,1)}, u32[]{:S(2)}, u32[]{:S(2)}) async-start(bf16[256,16,1,448]{0,3,2,1:T(8,128)(2,1)} %bitcast.58), calls=%async_computation.2 | async-start | bytes 7340032 | tf_op jit(solution)/shard_map/all_to_all | solution.py:70
  127.2 22.1 %copy-start = (bf16[56,8,16,256]{3,1,2,0:T(8,128)(2,1)}, bf16[56,8,16,256]{3,1,2,0:T(8,128)(2,1)S(1)}, u32[]{:S(2)}) copy-start(bf16[56,8,16,256]{3,1,2,0:T(8,128)(2,1)S(1)} %copy.73) | copy-start | bytes 11010052
  131.0 18.2 %copy-start.2 = (bf16[56,8,16,256]{3,1,2,0:T(8,128)(2,1)}, bf16[56,8,16,256]{3,1,2,0:T(8,128)(2,1)S(1)}, u32[]{:S(2)}) copy-start(bf16[56,8,16,256]{3,1,2,0:T(8,128)(2,1)S(1)} %copy.72) | copy-start | bytes 11010052
  163.3 108.5 %all-to-all-start.4 = ((bf16[8,2,2,16,2,3584]{5,0,4,2,1,3:T(8,128)(2,1)}), bf16[8,2,2,16,2,3584]{5,0,4,2,1,3:T(8,128)(2,1)}, u32[]{:S(2)}, u32[]{:S(2)}) async-start(bf16[8,2,2,16,2,3584]{5,0,4,2,1,3:T(8,128)(2,1)} %copy.64), calls=%async_computation.4 | async-start | bytes 14680064 | tf_op jit(solution)/shard_map/all_to_all | solution.py:101
  169.0 2.7 copy-start.5
  169.0 2.7 copy-start.6
  172.1 2.0 copy-start.1
  172.1 3.2 copy-start.3
  179.2 1.9 copy-start.4
  191.2 3.2 slice-start.4
  191.2 3.5 slice-start.6
  192.7 2.3 slice-start.5
  192.8 2.6 slice-start.7
  212.1 6.2 %slice-start = ((s8[7340032]{0:T(1024)(128)(4,1)}), s8[4194304]{0:T(1024)(128)(4,1)S(1)}, s32[]{:S(2)}) async-start(s8[7340032]{0:T(1024)(128)(4,1)} %bitcast.64), calls=%async_computation.6 | async-start | bytes 8388608
  212.1 6.2 %slice-start.2 = ((s8[7340032]{0:T(1024)(128)(4,1)}), s8[4194304]{0:T(1024)(128)(4,1)S(1)}, s32[]{:S(2)}) async-start(s8[7340032]{0:T(1024)(128)(4,1)} %bitcast.66), calls=%async_computation.8 | async-start | bytes 8388608
  212.1 6.2 %slice-start.1 = ((s8[7340032]{0:T(1024)(128)(4,1)}), s8[3145728]{0:T(1024)(128)(4,1)S(1)}, s32[]{:S(2)}) async-start(s8[7340032]{0:T(1024)(128)(4,1)} %bitcast.64), calls=%async_computation.7 | async-start | bytes 6291456
  212.1 6.2 %slice-start.3 = ((s8[7340032]{0:T(1024)(128)(4,1)}), s8[3145728]{0:T(1024)(128)(4,1)S(1)}, s32[]{:S(2)}) async-start(s8[7340032]{0:T(1024)(128)(4,1)} %bitcast.66), calls=%async_computation.9 | async-start | bytes 6291456
  271.8 52.8 %all-to-all-start.3 = ((bf16[16,2,57344]{2,1,0:T(2,128)(2,1)}), bf16[16,2,57344]{2,1,0:T(2,128)(2,1)}, u32[]{:S(2)}, u32[]{:S(2)}) async-start(bf16[16,2,57344]{2,1,0:T(2,128)(2,1)} %reshape.155), calls=%async_computation.3 | async-start | bytes 7340032 | tf_op jit(solution)/shard_map/all_to_all | solution.py:74
  324.5 87.5 %all-to-all-start.5 = ((bf16[8,2,2,16,2,3584]{5,4,3,2,1,0:T(2,128)(2,1)}), bf16[8,2,2,16,2,3584]{5,4,3,2,1,0:T(2,128)(2,1)}, u32[]{:S(2)}, u32[]{:S(2)}) async-start(bf16[8,2,2,16,2,3584]{5,4,3,2,1,0:T(2,128)(2,1)} %copy.65), calls=%async_computation.5 | async-start | bytes 14680064 | tf_op jit(solution)/shard_map/all_to_all | solution.py:100
where the time goes:
time: 427 us; the launch traced here: 420 us
  waiting for transfers between devices  153 us (36%)
  local copies, waits for them, and re-layouts  121 us (28%)
  matrix products  74.7 us (17%)
  starting transfers between devices  38.4 us (9%)
  other arithmetic  32.1 us (8%)
    unnamed x46, local copies, waits for them, and re-layouts  82.9 us
    all_to_all x1, waiting for transfers between devices, relocate(): lax.all_to_all(lax.all_to_all(outgoing, 'tok', split_axis=3, concat_axis=...  43.8 us
    dot_general x16, matrix products, attend_item(): lax.dot_general(query_block, key_block, (((1,), (1,)), ((), ())), preferr...  41.7 us
    all_to_all x1, waiting for transfers between devices, regroup_attend(): lax.all_to_all(by_group(key_rows), 'tok', split_axis=1, concat_axis=0, ti...  39.6 us
    all_to_all x1, waiting for transfers between devices, regroup_attend(): lax.all_to_all(mixed, 'tok', split_axis=0, concat_axis=1, tiled=True)  33.7 us
    all_to_all x1, waiting for transfers between devices, regroup_attend(): lax.all_to_all(by_group(query_rows), 'tok', split_axis=1, concat_axis=0,...  26.1 us
    dot_general x16, matrix products, attend_item(): jnp.dot(weights.astype(jnp.bfloat16), value_block, preferred_element_type...  25.8 us
    reduce_sum x8, other arithmetic, attend_item(): row_total = jnp.sum(weights, axis=1, keepdims=True)  19.1 us
  transfers between devices with their start and end apart: 6, of which 5 were waited for; matrix products, arithmetic and copies ran while one was open for 50% of the time, Pallas kernels for 0%

commit v1 on v0

--- a/solution.py
+++ b/solution.py
@@ -71,7 +71,10 @@
         ),
         segments=segments,
     )
-    returned = lax.all_to_all(mixed, "tok", split_axis=0, concat_axis=1, tiled=True)
+    returned = jnp.concatenate(
+        lax.all_to_all(jnp.stack(jnp.split(mixed, lax.axis_size("tok"), axis=0)), "tok", 0, 0),
+        axis=1,
+    )
     return returned.reshape(1, token_rows, feature_width)
 
 

time: 427 us -> 409 us (0.958)
  local copies, waits for them, and re-layouts: 121 us -> 64.7 us
  waiting for transfers between devices: 153 us -> 187 us
  other arithmetic: 32.1 us -> 38.1 us
    unnamed x46, local copies, waits for them, and re-layouts: 82.9 us -> 45.2 us
    all_to_all x1, waiting for transfers between devices: 43.8 us -> 76.7 us  [relocate(): lax.all_to_all(lax.all_to_all(outgoing, 'tok', split_axis=3, concat_axis=...]
    all_to_all x2 -> x0, local copies, waits for them, and re-layouts: 12.9 us -> none  [regroup_attend(): lax.all_to_all(mixed, 'tok', split_axis=0, concat_axis=1, tiled=True)]
    reduce_sum x8, other arithmetic: 19.1 us -> 26.3 us  [attend_item(): row_total = jnp.sum(weights, axis=1, keepdims=True)]
    another operation x2, other arithmetic: 6.34 us -> 0.89 us  [the longest x1 0.71 us: regroup_attend(): jnp.stack(jnp.split(mixed, lax.axis_size('tok'), axis=0))]
    dot_general x1, matrix products: 7.13 us -> 2.04 us  [relocate(): jnp.einsum('bdc,bjthy->dcjthy', placing, local_blocks, preferred_element_...]
    unnamed x11 -> x20, other arithmetic: 5.59 us -> 10.6 us
  transfers between devices with their start and end apart: 6 -> 6, of which waited for: 5 -> 5; matrix products, arithmetic and copies ran while one was open for 50% -> 39% of each run, Pallas kernels for 0% -> 0%
where the time goes in v1:
time: 409 us; the launch traced here: 403 us
  waiting for transfers between devices  187 us (46%)
  matrix products  73.6 us (18%)
  local copies, waits for them, and re-layouts  64.7 us (16%)
  starting transfers between devices  38.1 us (9%)
  other arithmetic  38.1 us (9%)
    all_to_all x1, waiting for transfers between devices, relocate(): lax.all_to_all(lax.all_to_all(outgoing, 'tok', split_axis=3, concat_axis=...  76.7 us
    dot_general x16, matrix products, attend_item(): lax.dot_general(query_block, key_block, (((1,), (1,)), ((), ())), preferr...  45.6 us
    unnamed x46, local copies, waits for them, and re-layouts  45.2 us
    all_to_all x1, waiting for transfers between devices, regroup_attend(): lax.all_to_all(by_group(key_rows), 'tok', split_axis=1, concat_axis=0, ti...  39.6 us
    all_to_all x1, waiting for transfers between devices, regroup_attend(): lax.all_to_all(jnp.stack(jnp.split(mixed, lax.axis_size('tok'), axis=0)),...  33.7 us
    reduce_sum x8, other arithmetic, attend_item(): row_total = jnp.sum(weights, axis=1, keepdims=True)  26.3 us
    dot_general x16, matrix products, attend_item(): jnp.dot(weights.astype(jnp.bfloat16), value_block, preferred_element_type...  25.9 us
    all_to_all x1, waiting for transfers between devices, regroup_attend(): lax.all_to_all(by_group(query_rows), 'tok', split_axis=1, concat_axis=0,...  24.9 us
  transfers between devices with their start and end apart: 6, of which 5 were waited for; matrix products, arithmetic and copies ran while one was open for 39% of the time, Pallas kernels for 0%

profile of v1, /device:TPU:1, one launch (start us, length us, event | category | flops | bytes accessed | tf_op | source)
XLA Modules:
  0.0 403.2 jit_solution(3388631596393671384)
XLA Ops:
  0.6 5.9 %copy.36 = bf16[1,256,7168]{1,2,0:T(8,128)(2,1)} copy(bf16[1,256,7168]{2,1,0:T(8,128)(2,1)} %param.7) | data formatting | bytes 7340032 | tf_op args[1]
  6.5 9.3 %all-to-all-start.1 = ((bf16[256,16,1,448]{0,3,2,1:T(8,128)(2,1)}), bf16[256,16,1,448]{0,3,2,1:T(8,128)(2,1)}, u32[]{:S(2)}, u32[]{:S(2)}) async-start(bf16[256,16,1,448]{0,3,2,1:T(8,128)(2,1)} %bitcast.140), calls=%async_computation.1 | async-start | bytes 7340032 | tf_op jit(solution)/shard_map/all_to_all | solution.py:69
  15.8 5.9 %copy.33 = bf16[1,256,7168]{1,2,0:T(8,128)(2,1)} copy(bf16[1,256,7168]{2,1,0:T(8,128)(2,1)} %param.6) | data formatting | bytes 7340032 | tf_op args[0]
  21.7 39.6 %all-to-all-done.1 = bf16[256,16,1,448]{0,3,2,1:T(8,128)(2,1)} async-done(((bf16[256,16,1,448]{0,3,2,1:T(8,128)(2,1)}), bf16[256,16,1,448]{0,3,2,1:T(8,128)(2,1)}, u32[]{:S(2)}, u32[]{:S(2)}) %all-to-all-start.1) | async-done | bytes 3670048 | tf_op jit(solution)/shard_map/all_to_all | solution.py:69
  61.3 5.3 %all-to-all-start = ((bf16[256,16,1,448]{0,3,2,1:T(8,128)(2,1)}), bf16[256,16,1,448]{0,3,2,1:T(8,128)(2,1)}, u32[]{:S(2)}, u32[]{:S(2)}) async-start(bf16[256,16,1,448]{0,3,2,1:T(8,128)(2,1)} %bitcast.139), calls=%async_computation | async-start | bytes 7340032 | tf_op jit(solution)/shard_map/all_to_all | solution.py:68
  67.0 5.9 %copy.39 = bf16[1,256,7168]{1,2,0:T(8,128)(2,1)} copy(bf16[1,256,7168]{2,1,0:T(8,128)(2,1)} %param.8) | data formatting | bytes 7340032 | tf_op args[2]
  72.9 4.1 %copy.47 = bf16[1,8,2,32,3584]{4,1,3,2,0:T(8,128)(2,1)S(1)} copy(bf16[1,8,2,32,3584]{4,3,2,1,0:T(8,128)(2,1)} %param.10) | data formatting | bytes 7340032 | tf_op jit(solution)/shard_map/reshape;squeeze | solution.py:97
  77.1 2.0 convolution_convert_fusion
  79.2 3.6 copy.43
  82.9 4.4 %copy.50 = bf16[56,8,16,256]{3,1,2,0:T(8,128)(2,1)} copy(bf16[56,8,16,256]{3,1,0,2:T(8,128)(2,1)} %bitcast.112) | data formatting | bytes 7340032
  87.3 24.9 %all-to-all-done = bf16[256,16,1,448]{0,3,2,1:T(8,128)(2,1)} async-done(((bf16[256,16,1,448]{0,3,2,1:T(8,128)(2,1)}), bf16[256,16,1,448]{0,3,2,1:T(8,128)(2,1)}, u32[]{:S(2)}, u32[]{:S(2)}) %all-to-all-start) | async-done | bytes 3670048 | tf_op jit(solution)/shard_map/all_to_all | solution.py:68
  112.2 5.5 %all-to-all-start.2 = ((bf16[256,16,1,448]{0,3,2,1:T(8,128)(2,1)}), bf16[256,16,1,448]{0,3,2,1:T(8,128)(2,1)}, u32[]{:S(2)}, u32[]{:S(2)}) async-start(bf16[256,16,1,448]{0,3,2,1:T(8,128)(2,1)} %bitcast.138), calls=%async_computation.2 | async-start | bytes 7340032 | tf_op jit(solution)/shard_map/all_to_all | solution.py:70
  117.7 2.7 copy.49
  123.2 2.6 fusion.343
  125.8 2.6 fusion.344
  128.5 2.7 fusion.219
  131.2 3.7 fusion.85
  134.9 3.4 fusion.345
  138.3 3.5 fusion.346
  141.8 4.5 %fusion.347 = (f32[512]{0:T(512)S(1)}, f32[512,3584]{1,0:T(8,128)}) fusion(bf16[4096,448]{0,1:T(8,128)(2,1)S(1)} %bitcast.131, bf16[4096,448]{0,1:T(8,128)(2,1)S(1)} %bitcast.155, s32[3584]{0:T(1024)S(1)} %iota_add_fusion, s32[512]{0:T(512)S(1)} %iota_add_fusion.7, s32[3584]{0:T(1024)S(1)} %bitcast.182, s32[512]{0:T(512)S(1)} %get-tuple-element.35), kind=kOutput, calls=%fused_computation.338 | convolution fusion | flops 833093120 | bytes 9213952 | tf_op jit(solution)/shard_map/dot_general | solution.py:34
  146.3 4.5 %fusion.348 = (f32[512]{0:T(512)S(1)}, f32[512,3584]{1,0:T(8,128)}) fusion(bf16[4096,448]{0,1:T(8,128)(2,1)S(1)} %bitcast.132, bf16[4096,448]{0,1:T(8,128)(2,1)S(1)} %bitcast.156, s32[3584]{0:T(1024)S(1)} %iota_add_fusion, s32[512]{0:T(512)S(1)} %iota_add_fusion.7, s32[3584]{0:T(1024)S(1)} %bitcast.183, s32[512]{0:T(512)S(1)} %get-tuple-element.35), kind=kOutput, calls=%fused_computation.339 | convolution fusion | flops 833093120 | bytes 9213952 | tf_op jit(solution)/shard_map/dot_general | solution.py:34
  150.8 12.4 %all-to-all-done.2 = bf16[256,16,1,448]{0,3,2,1:T(8,128)(2,1)} async-done(((bf16[256,16,1,448]{0,3,2,1:T(8,128)(2,1)}), bf16[256,16,1,448]{0,3,2,1:T(8,128)(2,1)}, u32[]{:S(2)}, u32[]{:S(2)}) %all-to-all-start.2) | async-done | bytes 3670048 | tf_op jit(solution)/shard_map/all_to_all | solution.py:70
  163.1 5.9 %all-to-all-start.4 = ((bf16[8,2,2,16,2,3584]{5,0,4,2,1,3:T(8,128)(2,1)}), bf16[8,2,2,16,2,3584]{5,0,4,2,1,3:T(8,128)(2,1)}, u32[]{:S(2)}, u32[]{:S(2)}) async-start(bf16[8,2,2,16,2,3584]{5,0,4,2,1,3:T(8,128)(2,1)} %copy.43), calls=%async_computation.4 | async-start | bytes 14680064 | tf_op jit(solution)/shard_map/all_to_all | solution.py:104
  169.0 2.6 copy.48
  174.4 2.0 fusion.62
  182.1 2.1 fusion.55
  187.9 3.0 fusion.18
  190.8 3.4 fusion.51
  198.8 3.2 fusion.29
  205.3 3.8 fusion.4
  209.1 4.8 %fusion.33 = (f32[512]{0:T(512)S(1)}, f32[512]{0:T(512)S(1)}) fusion(f32[512,3072]{1,0:T(8,128)S(1)} %get-tuple-element.56, f32[512]{0:T(512)S(1)} %get-tuple-element.14, s32[3072]{0:T(1024)S(1)} %iota_add_fusion.1, s32[512]{0:T(512)S(1)} %iota_add_fusion.8, s32[3072]{0:T(1024)S(1)} %slice.378, s32[512]{0:T(512)S(1)} %get-tuple-element.36, ...), kind=kLoop, calls=%fused_computation.55 | loop fusion | flops 20446208 | bytes 12619776 | tf_op jit(solution)/shard_map/reduce_sum | solution.py:40
  213.9 2.2 fusion.116
  216.1 2.2 fusion.126
  221.3 4.3 %fusion.7 = (f32[512]{0:T(512)S(1)}, f32[512]{0:T(512)S(1)}) fusion(f32[512,3584]{1,0:T(8,128)S(1)} %bitcast.143, f32[512]{0:T(512)S(1)} %get-tuple-element.59, s32[3584]{0:T(1024)S(1)} %iota_add_fusion, s32[512]{0:T(512)S(1)} %iota_add_fusion.7, s32[3584]{0:T(1024)S(1)} %bitcast.184, s32[512]{0:T(512)S(1)} %get-tuple-element.35, ...), kind=kLoop, calls=%fused_computation.28 | loop fusion | flops 16514048 | bytes 14721024 | tf_op jit(solution)/shard_map/reduce_sum | solution.py:40
  225.6 2.2 fusion.136
  230.6 2.1 fusion.146
  234.2 2.2 fusion.67
  236.5 4.7 %fusion.2 = (f32[512]{0:T(512)S(1)}, f32[512]{0:T(512)S(1)}, f32[512,4096]{1,0:T(8,128)S(1)}) fusion(s32[512]{0:T(512)S(1)} %iota_add_fusion.6, s32[4096]{0:T(1024)S(1)} %convert_reduce_fusion, s32[512]{0:T(512)S(1)} %get-tuple-element.34, f32[512,4096]{1,0:T(8,128)S(1)} %fusion.67, bf16[4096,448]{0,1:T(8,128)(2,1)S(1)} %bitcast.137, ...), kind=kOutput, calls=%fused_computation.8 | convolution fusion | flops 958397440 | bytes 18866176 | tf_op jit(solution)/shard_map/dot_general | solution.py:34
  241.2 6.4 %fusion.11 = (f32[512]{0:T(512)S(1)}, f32[512]{0:T(512)S(1)}) fusion(f32[512,4096]{1,0:T(8,128)S(1)} %get-tuple-element.61, f32[512]{0:T(512)S(1)} %get-tuple-element.20, s32[512]{0:T(512)S(1)} %iota_add_fusion.6, s32[4096]{0:T(1024)S(1)} %convert_reduce_fusion, s32[512]{0:T(512)S(1)} %get-tuple-element.34, f32[512]{0:T(512)S(1)} %get-tuple-element.21, ...), kind=kLoop, calls=%fused_computation.32 | loop fusion | flops 27261952 | bytes 16805888 | tf_op jit(solution)/shard_map/reduce_sum | solution.py:40
  247.6 3.0 fusion.156
  250.6 3.0 fusion.166
  255.0 7.3 %all-to-all-start.3 = ((bf16[16,256,1,1,448]{1,4,3,2,0:T(8,128)(2,1)}), bf16[16,256,1,1,448]{1,4,3,2,0:T(8,128)(2,1)}, u32[]{:S(2)}, u32[]{:S(2)}) async-start(bf16[16,256,1,1,448]{1,4,3,2,0:T(8,128)(2,1)} %fusion.266), calls=%async_computation.3 | async-start | bytes 7340032 | tf_op jit(solution)/shard_map/all_to_all | solution.py:75
  262.2 11.8 %copy.44 = bf16[8,2,2,16,2,3584]{5,4,3,2,1,0:T(2,128)(2,1)} copy(bf16[8,2,2,16,2,3584]{5,0,4,2,1,3:T(8,128)(2,1)} %all-to-all-done.4) | data formatting | bytes 14680064 | tf_op jit(solution)/shard_map/all_to_all | solution.py:104
  274.1 33.7 %all-to-all-done.3 = bf16[16,256,1,1,448]{1,4,3,2,0:T(8,128)(2,1)} async-done(((bf16[16,256,1,1,448]{1,4,3,2,0:T(8,128)(2,1)}), bf16[16,256,1,1,448]{1,4,3,2,0:T(8,128)(2,1)}, u32[]{:S(2)}, u32[]{:S(2)}) %all-to-all-start.3) | async-done | bytes 3670048 | tf_op jit(solution)/shard_map/all_to_all | solution.py:75
  307.7 4.8 %all-to-all-start.5 = ((bf16[8,2,2,16,2,3584]{5,4,3,2,1,0:T(2,128)(2,1)}), bf16[8,2,2,16,2,3584]{5,4,3,2,1,0:T(2,128)(2,1)}, u32[]{:S(2)}, u32[]{:S(2)}) async-start(bf16[8,2,2,16,2,3584]{5,4,3,2,1,0:T(2,128)(2,1)} %copy.44), calls=%async_computation.5 | async-start | bytes 14680064 | tf_op jit(solution)/shard_map/all_to_all | solution.py:103
  312.6 5.9 %copy.45 = bf16[1,256,7168]{2,1,0:T(8,128)(2,1)} copy(bf16[1,256,7168]{1,2,0:T(8,128)(2,1)} %bitcast.31) | data formatting | bytes 7340032
  318.5 76.7 %all-to-all-done.5 = bf16[8,2,2,16,2,3584]{5,4,3,2,1,0:T(2,128)(2,1)} async-done(((bf16[8,2,2,16,2,3584]{5,4,3,2,1,0:T(2,128)(2,1)}), bf16[8,2,2,16,2,3584]{5,4,3,2,1,0:T(2,128)(2,1)}, u32[]{:S(2)}, u32[]{:S(2)}) %all-to-all-start.5) | async-done | bytes 7340064 | tf_op jit(solution)/shard_map/all_to_all | solution.py:103
  395.2 7.6 %copy.70 = bf16[1,8,2,2,16,2,3584]{6,5,4,3,2,1,0:T(2,128)(2,1)} copy(bf16[1,8,2,2,16,2,3584]{6,5,4,3,2,1,0:T(2,128)(2,1)} %bitcast.37) | data formatting | bytes 14680064
  (100 shorter events, 32.0 us)
Async XLA Ops:
  6.5 54.8 %all-to-all-start.1 = ((bf16[256,16,1,448]{0,3,2,1:T(8,128)(2,1)}), bf16[256,16,1,448]{0,3,2,1:T(8,128)(2,1)}, u32[]{:S(2)}, u32[]{:S(2)}) async-start(bf16[256,16,1,448]{0,3,2,1:T(8,128)(2,1)} %bitcast.140), calls=%async_computation.1 | async-start | bytes 7340032 | tf_op jit(solution)/shard_map/all_to_all | solution.py:69
  61.3 5.3 %copy-start.7 = (s32[1,6]{1,0:T(1,128)S(1)}, s32[1,6]{1,0:T(1,128)}, u32[]{:S(2)}) copy-start(s32[1,6]{1,0:T(1,128)} %param.9) | copy-start | bytes 76
  61.3 50.9 %all-to-all-start = ((bf16[256,16,1,448]{0,3,2,1:T(8,128)(2,1)}), bf16[256,16,1,448]{0,3,2,1:T(8,128)(2,1)}, u32[]{:S(2)}, u32[]{:S(2)}) async-start(bf16[256,16,1,448]{0,3,2,1:T(8,128)(2,1)} %bitcast.139), calls=%async_computation | async-start | bytes 7340032 | tf_op jit(solution)/shard_map/all_to_all | solution.py:68
  72.9 4.1 %copy-start.8 = (s32[1,8,1]{1,2,0:T(1,128)S(1)}, s32[1,8,1]{1,2,0:T(1,128)}, u32[]{:S(2)}) copy-start(s32[1,8,1]{1,2,0:T(1,128)} %param.11) | copy-start | bytes 100
  112.2 50.9 %all-to-all-start.2 = ((bf16[256,16,1,448]{0,3,2,1:T(8,128)(2,1)}), bf16[256,16,1,448]{0,3,2,1:T(8,128)(2,1)}, u32[]{:S(2)}, u32[]{:S(2)}) async-start(bf16[256,16,1,448]{0,3,2,1:T(8,128)(2,1)} %bitcast.138), calls=%async_computation.2 | async-start | bytes 7340032 | tf_op jit(solution)/shard_map/all_to_all | solution.py:70
  117.7 3.1 copy-start
  120.4 25.9 %copy-start.3 = (bf16[56,8,16,256]{3,1,2,0:T(8,128)(2,1)}, bf16[56,8,16,256]{3,1,2,0:T(8,128)(2,1)S(1)}, u32[]{:S(2)}) copy-start(bf16[56,8,16,256]{3,1,2,0:T(8,128)(2,1)S(1)} %copy.49) | copy-start | bytes 11010052
  163.1 91.8 %all-to-all-start.4 = ((bf16[8,2,2,16,2,3584]{5,0,4,2,1,3:T(8,128)(2,1)}), bf16[8,2,2,16,2,3584]{5,0,4,2,1,3:T(8,128)(2,1)}, u32[]{:S(2)}, u32[]{:S(2)}) async-start(bf16[8,2,2,16,2,3584]{5,0,4,2,1,3:T(8,128)(2,1)} %copy.43), calls=%async_computation.4 | async-start | bytes 14680064 | tf_op jit(solution)/shard_map/all_to_all | solution.py:104
  169.0 2.6 copy-start.6
  172.1 2.3 copy-start.1
  179.1 2.4 copy-start.4
  179.1 3.0 copy-start.5
  185.3 2.5 copy-start.2
  194.2 4.6 %slice-start.6 = ((s8[5242880]{0:T(1024)(128)(4,1)}), s8[1048576]{0:T(1024)(128)(4,1)S(1)}, s32[]{:S(2)}) async-start(s8[5242880]{0:T(1024)(128)(4,1)} %bitcast.162), calls=%async_computation.12 | async-start | bytes 2097152
  194.2 4.6 %slice-start.8 = ((s8[5242880]{0:T(1024)(128)(4,1)}), s8[4194304]{0:T(1024)(128)(4,1)S(1)}, s32[]{:S(2)}) async-start(s8[5242880]{0:T(1024)(128)(4,1)} %bitcast.164), calls=%async_computation.14 | async-start | bytes 8388608
  195.8 3.0 slice-start.7
  195.8 3.0 slice-start.9
  202.0 3.3 slice-start
  203.6 1.7 slice-start.1
  216.1 2.2 slice-start.2
  216.1 3.5 slice-start.4
  216.1 4.3 %slice-start.3 = ((s8[7340032]{0:T(1024)(128)(4,1)}), s8[3145728]{0:T(1024)(128)(4,1)S(1)}, s32[]{:S(2)}) async-start(s8[7340032]{0:T(1024)(128)(4,1)} %bitcast.142), calls=%async_computation.9 | async-start | bytes 6291456
  216.1 5.2 %slice-start.5 = ((s8[7340032]{0:T(1024)(128)(4,1)}), s8[3145728]{0:T(1024)(128)(4,1)S(1)}, s32[]{:S(2)}) async-start(s8[7340032]{0:T(1024)(128)(4,1)} %bitcast.144), calls=%async_computation.11 | async-start | bytes 6291456
  255.0 52.7 %all-to-all-start.3 = ((bf16[16,256,1,1,448]{1,4,3,2,0:T(8,128)(2,1)}), bf16[16,256,1,1,448]{1,4,3,2,0:T(8,128)(2,1)}, u32[]{:S(2)}, u32[]{:S(2)}) async-start(bf16[16,256,1,1,448]{1,4,3,2,0:T(8,128)(2,1)} %fusion.266), calls=%async_computation.3 | async-start | bytes 7340032 | tf_op jit(solution)/shard_map/all_to_all | solution.py:75
  307.7 87.5 %all-to-all-start.5 = ((bf16[8,2,2,16,2,3584]{5,4,3,2,1,0:T(2,128)(2,1)}), bf16[8,2,2,16,2,3584]{5,4,3,2,1,0:T(2,128)(2,1)}, u32[]{:S(2)}, u32[]{:S(2)}) async-start(bf16[8,2,2,16,2,3584]{5,4,3,2,1,0:T(2,128)(2,1)} %copy.44), calls=%async_computation.5 | async-start | bytes 14680064 | tf_op jit(solution)/shard_map/all_to_all | solution.py:103
